TPU v7x, 32 devices: a whole 2x2x4 slice. The times are simulated.
32 devices in a mesh: blk: 16 (over z, y, core), grp: 2 (over x).
Axes of the slice: x: 2, y: 2, z: 4, core: 2. Of those that a mesh axis runs over, the one named last changes fastest.
Arguments:
- tracers: float32 [2, 16, 128, 256], P(None, None, 'blk', 'grp'), may hold values from -6 to 6
- velocity: float32 [2, 16, 128, 256], P(None, None, 'blk', 'grp'), may hold values from -3 to 3
- depth_levels: int32 [128, 256], P('blk', 'grp'), may hold values from 0 to 16, as said below
- vdiff: float32 [15], replicated, may hold values from 0.05 to 0.45
Outputs:
- new_tracers: float32 [2, 16, 128, 256], P(None, None, 'blk', 'grp')
- surface: float32 [128, 256], P('blk', 'grp')
- residual: float32 [128, 256], P('blk', 'grp')
Inputs may be any that keep to these rules, and one draw needn't show every extreme that they name: `depth_levels`: 16 and 0 are both reached in every draw.
All inputs are finite; a program needn't handle non-finite values.
Results may differ from a plain program's by a relative error of at most 0.0003.
Values sent between devices are 32-bit elements; how exact they have to be, the bound alone decides.
No kernel may reach another device: no remote copies, remote signals or barrier semaphores. Data moves between devices by JAX's collectives and lax.ppermute only.
A program may use at most 64 MiB of HBM per device.

v0:
```python
import jax
import jax.numpy as jnp
from jax import lax
from jax.sharding import PartitionSpec as P

ITERS = 3
TIME_STEP = 0.2
MIX_COEF = 0.25
SEA_DIAG = 0.5


def swapped(value, axis, stride):
    return lax.ppermute(value, axis, [(i, i ^ 1 << stride) for i in range(lax.axis_size(axis))])


def padded_2(cells, sides, width, closed):
    for axis, dim in sides:
        count = lax.axis_size(axis)
        ends = count if closed else count - 1
        head = lax.slice_in_dim(cells, 0, width, axis=dim)
        tail = lax.slice_in_dim(cells, cells.shape[dim] - width, cells.shape[dim], axis=dim)
        cells = jnp.concatenate(
            [
                lax.ppermute(tail, axis, [(i, (i + 1) % count) for i in range(ends)]),
                cells,
                lax.ppermute(head, axis, [((i + 1) % count, i) for i in range(ends)]),
            ],
            axis=dim,
        )
    return cells


def tracer_step(tracer, velocity, depth_pad, vdiff):
    count = tracer.shape[1]
    levels = jnp.arange(count, dtype=jnp.float32)[:, None, None]
    wet_mask = (levels < depth_pad[None]).astype(jnp.float32)
    east_vel = velocity[0]
    north_vel = velocity[1]
    row_set = tracer[:, :, 1:-1, :]
    wet_rows = wet_mask[:, 1:-1, :]
    east_rows = east_vel[:, 1:-1, :]
    east_open = wet_rows[:, :, :-1] * wet_rows[:, :, 1:]
    east_face = 0.5 * (east_rows[:, :, :-1] + east_rows[:, :, 1:])
    east_flux = east_open * (
        east_face * 0.5 * (row_set[..., :-1] + row_set[..., 1:])
        - MIX_COEF * (row_set[..., 1:] - row_set[..., :-1])
    )
    col_set = tracer[:, :, :, 1:-1]
    wet_cols = wet_mask[:, :, 1:-1]
    north_cols = north_vel[:, :, 1:-1]
    north_open = wet_cols[:, :-1, :] * wet_cols[:, 1:, :]
    north_face = 0.5 * (north_cols[:, :-1, :] + north_cols[:, 1:, :])
    north_flux = north_open * (
        north_face * 0.5 * (col_set[:, :, :-1, :] + col_set[:, :, 1:, :])
        - MIX_COEF * (col_set[:, :, 1:, :] - col_set[:, :, :-1, :])
    )
    centre = tracer[:, :, 1:-1, 1:-1]
    wet_centre = wet_mask[:, 1:-1, 1:-1]
    vert_open = wet_centre[:-1] * wet_centre[1:]
    vert_flux = vdiff[:, None, None] * vert_open * (centre[:, 1:] - centre[:, :-1])
    border = jnp.zeros_like(centre[:, :1])
    vert_flux = jnp.concatenate([border, vert_flux, border], 1)
    tendency = (
        vert_flux[:, 1:]
        - vert_flux[:, :-1]
        - (east_flux[..., 1:] - east_flux[..., :-1])
        - (north_flux[:, :, 1:, :] - north_flux[:, :, :-1, :])
    )
    return wet_centre * (centre + TIME_STEP * tendency)


def column_forcing(velocity, depth_pad):
    count = velocity.shape[1]
    levels = jnp.arange(count, dtype=jnp.float32)[:, None, None]
    wet_mask = (levels < depth_pad[None]).astype(jnp.float32)
    east_sum = jnp.sum(wet_mask * velocity[0], 0)
    north_sum = jnp.sum(wet_mask * velocity[1], 0)
    ocean_mask = (depth_pad[1:-1, 1:-1] > 0).astype(jnp.float32)
    return ocean_mask * (
        0.5 * (east_sum[1:-1, 2:] - east_sum[1:-1, :-2])
        + 0.5 * (north_sum[2:, 1:-1] - north_sum[:-2, 1:-1])
    )


def sea_operator(field_pad, depth_pad, count):
    centre = field_pad[1:-1, 1:-1]
    depth_c = depth_pad[1:-1, 1:-1]
    ocean_mask = (depth_c > 0).astype(jnp.float32)
    total = SEA_DIAG * centre
    for rows_at, cols_at in (
        (slice(1, -1), slice(2, None)),
        (slice(1, -1), slice(None, -2)),
        (slice(2, None), slice(1, -1)),
        (slice(None, -2), slice(1, -1)),
    ):
        weight = jnp.minimum(depth_c, depth_pad[rows_at, cols_at]) / count
        total = total + weight * (centre - field_pad[rows_at, cols_at])
    return ocean_mask * total + (1.0 - ocean_mask) * centre


def extend(fields, fold_sign):
    top_row = fields[:, -1, :]
    partner = top_row
    for bit_index in range(lax.axis_size("grp").bit_length() - 1):
        partner = swapped(partner, "grp", bit_index)
    mirror = partner[:, ::-1]
    northmost = lax.axis_index("blk") == lax.axis_size("blk") - 1
    row_halo = padded_2(fields, (("blk", 1),), 1, False)
    north_row = jnp.where(northmost, mirror * fold_sign[:, None], row_halo[:, -1, :])
    grown = jnp.concatenate([row_halo[:, :-1, :], north_row[:, None, :]], 1)
    return padded_2(grown, (("grp", 2),), 1, True)


def two_sums(residual, applied):
    return lax.psum((jnp.sum(residual * residual), jnp.sum(residual * applied)), ("blk", "grp"))


def shards(tracers, velocity, depth_levels, vdiff):
    count = tracers.shape[1]
    height, breadth = depth_levels.shape
    fields = jnp.concatenate(
        [
            tracers.reshape(2 * count, height, breadth),
            velocity.reshape(2 * count, height, breadth),
            depth_levels.astype(jnp.float32)[None],
        ],
        0,
    )
    fold_sign = jnp.concatenate(
        [
            jnp.ones((2 * count,), jnp.float32),
            -jnp.ones((2 * count,), jnp.float32),
            jnp.ones((1,), jnp.float32),
        ]
    )
    padded = extend(fields, fold_sign)
    tracer_pad = padded[: 2 * count].reshape(2, count, height + 2, breadth + 2)
    velocity_pad = padded[2 * count : 4 * count].reshape(2, count, height + 2, breadth + 2)
    depth_pad = padded[4 * count]
    new_tracers = tracer_step(tracer_pad, velocity_pad, depth_pad, vdiff)
    forcing = column_forcing(velocity_pad, depth_pad)

    def apply_op(field):
        grown = extend(field[None], jnp.ones((1,), jnp.float32))[0]
        return sea_operator(grown, depth_pad, count)

    surface = jnp.zeros_like(forcing)
    residual = forcing
    applied = apply_op(residual)
    norm_now, product = two_sums(residual, applied)
    step_len = norm_now / product
    direction, along = (residual, applied)
    for sweep in range(ITERS):
        surface = surface + step_len * direction
        residual = residual - step_len * along
        if sweep + 1 < ITERS:
            applied = apply_op(residual)
            norm_next, product = two_sums(residual, applied)
            beta_ratio = norm_next / norm_now
            step_len = norm_next / (product - beta_ratio * norm_next / step_len)
            direction = residual + beta_ratio * direction
            along = applied + beta_ratio * along
            norm_now = norm_next
    return (new_tracers, surface, residual)


def solution(mesh):
    return jax.shard_map(
        shards,
        mesh=mesh,
        in_specs=(P(None, None, "blk", "grp"), P(None, None, "blk", "grp"), P("blk", "grp"), P()),
        out_specs=(P(None, None, "blk", "grp"), P("blk", "grp"), P("blk", "grp")),
        check_vma=False,
    )
```

profile of v0, /device:TPU:0, one launch (start us, length us, event | category | flops | bytes accessed | tf_op | source)
XLA Modules:
  0.0 197.3 jit_solution(13682118741915809105)
XLA Ops:
  0.6 0.7 convert_bitcast_fusion
  1.3 1.1 pad_maximum_fusion.20
  2.5 3.0 %collective-permute-start.1 = (f32[65,128]{1,0:T(8,128)S(1)}, f32[65,128]{1,0:T(8,128)S(1)}, u32[]{:S(2)}, u32[]{:S(2)}) collective-permute-start(f32[65,128]{1,0:T(8,128)S(1)} %bitcast.70), channel_id=1, source_target_pairs={{0,1},{1,0},{2,3},{3,2},{4,5},{5,4},{6,7},{7,6},{8,9},{9,8},{10,11... | collective-permute-start | bytes 99848 | tf_op jit(solution)/shard_map/ppermute | solution.py:13
  5.5 1.3 collective-permute-start.2
  6.8 3.0 %collective-permute-start = (f32[65,1,128]{2,1,0:T(1,128)S(1)}, f32[65,1,128]{2,1,0:T(1,128)S(1)}, u32[]{:S(2)}, u32[]{:S(2)}) collective-permute-start(f32[65,1,128]{2,1,0:T(1,128)S(1)} %get-tuple-element.27), channel_id=1, source_target_pairs={{0,2},{2,4},{4,6},{6,8},{8,10},{10,12},{12,14},{14,16},{16,18},{18... | collective-permute-start | bytes 99848 | tf_op jit(solution)/shard_map/ppermute | solution.py:24
  9.9 0.7 fusion.14
  10.7 1.1 pad_maximum_fusion.1
  11.8 0.2 fusion.58
  12.0 0.2 copy.30
  12.2 0.2 copy.31
  12.5 2.0 %collective-permute-start.3 = (f32[65,10,1]{0,2,1:T(1,128)S(1)}, f32[65,10,1]{0,2,1:T(1,128)S(1)}, u32[]{:S(2)}, u32[]{:S(2)}) collective-permute-start(f32[65,10,1]{0,2,1:T(1,128)S(1)} %copy.30), channel_id=1, source_target_pairs={{0,1},{1,0},{2,3},{3,2},{4,5},{5,4},{6,7},{7,6},{8,9},{9,8},{10,11... | collective-permute-start | bytes 7808 | tf_op jit(solution)/shard_map/ppermute | solution.py:24
  14.6 1.6 collective-permute-done.3
  16.2 0.3 copy.32
  16.5 0.3 copy.33
  16.9 0.1 maximum_bitcast_fusion
  17.0 0.1 slice_multiply_fusion
  17.1 0.1 slice_multiply_fusion.1
  17.2 0.4 fusion.1
  17.7 0.1 fusion.51
  17.8 2.2 %collective-permute-start.5 = (f32[1,1,128]{2,1,0:T(1,128)S(1)}, f32[1,1,128]{2,1,0:T(1,128)S(1)}, u32[]{:S(2)}, u32[]{:S(2)}) collective-permute-start(f32[1,1,128]{2,1,0:T(1,128)S(1)} %get-tuple-element.43), channel_id=1, source_target_pairs={{0,2},{2,4},{4,6},{6,8},{8,10},{10,12},{12,14},{14,16},{16,18},{18... | collective-permute-start | bytes 1544 | tf_op jit(solution)/shard_map/ppermute | solution.py:24
  19.9 1.9 collective-permute-start.6
  21.8 1.3 collective-permute-start.7
  23.1 0.8 pad_maximum_fusion
  23.9 0.2 copy.35
  24.1 0.1 fusion.11
  24.4 0.1 subtract_multiply_fusion.1
  24.6 0.1 subtract_multiply_fusion
  24.7 0.3 copy-done.2
  25.0 0.1 fusion.13
  25.1 0.1 rev.13
  25.2 2.3 %collective-permute-done.7 = f32[1,1,128]{2,1,0:T(1,128)S(1)} collective-permute-done((f32[1,1,128]{2,1,0:T(1,128)S(1)}, f32[1,1,128]{2,1,0:T(1,128)S(1)}, u32[]{:S(2)}, u32[]{:S(2)}) %collective-permute-start.7) | collective-permute-done | bytes 544 | tf_op jit(solution)/shard_map/ppermute | solution.py:26
  27.6 0.5 collective-permute-start.8
  28.2 1.5 collective-permute-start.9
  29.6 1.6 collective-permute-done.8
  31.3 0.5 collective-permute-done.9
  31.9 0.7 multiply_reduce_fusion.4
  32.6 43.7 %all-reduce.4 = (f32[]{:T(128)}, f32[]{:T(128)}) all-reduce(f32[]{:T(128)} %get-tuple-element.13, f32[]{:T(128)} %get-tuple-element.12), channel_id=1, replica_groups=mesh['blk'=16,'grp'=2] {'blk','grp'}, use_global_device_ids=true, to_apply=%region_3.4 | all-reduce | flops 2 | bytes 16 | tf_op jit(solution)/shard_map/psum | solution.py:115
  77.6 2.3 %collective-permute-start.11 = (f32[1,128]{1,0:T(1,128)S(1)}, f32[1,128]{1,0:T(1,128)S(1)}, u32[]{:S(2)}, u32[]{:S(2)}) collective-permute-start(f32[1,128]{1,0:T(1,128)S(1)} %get-tuple-element.41), channel_id=1, source_target_pairs={{0,1},{1,0},{2,3},{3,2},{4,5},{5,4},{6,7},{7,6},{8,9},{9,8},{10,11... | collective-permute-start | bytes 1544 | tf_op jit(solution)/shard_map/ppermute | solution.py:13
  80.0 1.3 collective-permute-start.12
  81.3 0.1 fusion.12
  81.4 0.1 slice.328
  81.5 3.0 %collective-permute-start.10 = (f32[1,1,128]{2,1,0:T(1,128)S(1)}, f32[1,1,128]{2,1,0:T(1,128)S(1)}, u32[]{:S(2)}, u32[]{:S(2)}) collective-permute-start(f32[1,1,128]{2,1,0:T(1,128)S(1)} %get-tuple-element.40), channel_id=1, source_target_pairs={{0,2},{2,4},{4,6},{6,8},{8,10},{10,12},{12,14},{14,16},{16,18},{18... | collective-permute-start | bytes 1544 | tf_op jit(solution)/shard_map/ppermute | solution.py:24
  84.6 0.1 rev.14
  84.7 0.7 collective-permute-done.10
  85.4 0.1 fusion.60
  85.5 2.0 %collective-permute-start.14 = (f32[1,10,1]{2,1,0:T(8,128)S(1)}, f32[1,10,1]{2,1,0:T(8,128)S(1)}, u32[]{:S(2)}, u32[]{:S(2)}) collective-permute-start(f32[1,10,1]{2,1,0:T(8,128)S(1)} %get-tuple-element.32), channel_id=1, source_target_pairs={{1,0},{0,1},{3,2},{2,3},{5,4},{4,5},{7,6},{6,7},{9,8},{8,9},{11,10... | collective-permute-start | bytes 128 | tf_op jit(solution)/shard_map/ppermute | solution.py:26
  87.5 1.6 collective-permute-done.13
  89.1 0.1 collective-permute-done.14
  89.3 0.7 multiply_reduce_fusion.2
  89.9 42.7 %all-reduce.3 = (f32[]{:T(128)}, f32[]{:T(128)}) all-reduce(f32[]{:T(128)} %get-tuple-element.11, f32[]{:T(128)} %get-tuple-element.10), channel_id=1, replica_groups=mesh['blk'=16,'grp'=2] {'blk','grp'}, use_global_device_ids=true, to_apply=%region_7.8 | all-reduce | flops 2 | bytes 16 | tf_op jit(solution)/shard_map/psum | solution.py:115
  137.4 2.3 %collective-permute-start.16 = (f32[1,128]{1,0:T(1,128)S(1)}, f32[1,128]{1,0:T(1,128)S(1)}, u32[]{:S(2)}, u32[]{:S(2)}) collective-permute-start(f32[1,128]{1,0:T(1,128)S(1)} %get-tuple-element.38), channel_id=1, source_target_pairs={{0,1},{1,0},{2,3},{3,2},{4,5},{5,4},{6,7},{7,6},{8,9},{9,8},{10,11... | collective-permute-start | bytes 1544 | tf_op jit(solution)/shard_map/ppermute | solution.py:13
  139.7 1.3 collective-permute-start.17
  141.0 0.1 fusion.6
  141.2 0.7 copy.44
  141.9 3.0 %collective-permute-start.15 = (f32[1,1,128]{2,1,0:T(1,128)S(1)}, f32[1,1,128]{2,1,0:T(1,128)S(1)}, u32[]{:S(2)}, u32[]{:S(2)}) collective-permute-start(f32[1,1,128]{2,1,0:T(1,128)S(1)} %get-tuple-element.37), channel_id=1, source_target_pairs={{0,2},{2,4},{4,6},{6,8},{8,10},{10,12},{12,14},{14,16},{16,18},{18... | collective-permute-start | bytes 1544 | tf_op jit(solution)/shard_map/ppermute | solution.py:24
  144.9 0.1 rev.15
  145.0 0.7 collective-permute-done.15
  145.7 0.1 fusion.59
  145.8 2.0 %collective-permute-start.19 = (f32[1,10,1]{2,1,0:T(8,128)S(1)}, f32[1,10,1]{2,1,0:T(8,128)S(1)}, u32[]{:S(2)}, u32[]{:S(2)}) collective-permute-start(f32[1,10,1]{2,1,0:T(8,128)S(1)} %get-tuple-element.30), channel_id=1, source_target_pairs={{1,0},{0,1},{3,2},{2,3},{5,4},{4,5},{7,6},{6,7},{9,8},{8,9},{11,10... | collective-permute-start | bytes 128 | tf_op jit(solution)/shard_map/ppermute | solution.py:26
  147.8 1.6 collective-permute-done.18
  149.5 0.1 collective-permute-done.19
  149.7 0.7 multiply_reduce_fusion
  150.4 42.3 %all-reduce.2 = (f32[]{:T(128)}, f32[]{:T(128)}) all-reduce(f32[]{:T(128)} %get-tuple-element.9, f32[]{:T(128)} %get-tuple-element.8), channel_id=1, replica_groups=mesh['blk'=16,'grp'=2] {'blk','grp'}, use_global_device_ids=true, to_apply=%region_11.12 | all-reduce | flops 2 | bytes 16 | tf_op jit(solution)/shard_map/psum | solution.py:115
  196.7 0.6 multiply_subtract_fusion
  (46 shorter events, 0.9 us)
Async XLA Ops:
  2.5 7.4 %collective-permute-start.1 = (f32[65,128]{1,0:T(8,128)S(1)}, f32[65,128]{1,0:T(8,128)S(1)}, u32[]{:S(2)}, u32[]{:S(2)}) collective-permute-start(f32[65,128]{1,0:T(8,128)S(1)} %bitcast.70), channel_id=1, source_target_pairs={{0,1},{1,0},{2,3},{3,2},{4,5},{5,4},{6,7},{7,6},{8,9},{9,8},{10,11... | collective-permute-start | bytes 99848 | tf_op jit(solution)/shard_map/ppermute | solution.py:13
  5.5 4.4 %collective-permute-start.2 = (f32[65,1,128]{2,0,1:T(8,128)S(1)}, f32[65,1,128]{2,0,1:T(8,128)S(1)}, u32[]{:S(2)}, u32[]{:S(2)}) collective-permute-start(f32[65,1,128]{2,0,1:T(8,128)S(1)} %copy.46), channel_id=1, source_target_pairs={{2,0},{4,2},{6,4},{8,6},{10,8},{12,10},{14,12},{16,14},{18,16},{20... | collective-permute-start | bytes 99848 | tf_op jit(solution)/shard_map/ppermute | solution.py:26
  6.8 3.9 %collective-permute-start = (f32[65,1,128]{2,1,0:T(1,128)S(1)}, f32[65,1,128]{2,1,0:T(1,128)S(1)}, u32[]{:S(2)}, u32[]{:S(2)}) collective-permute-start(f32[65,1,128]{2,1,0:T(1,128)S(1)} %get-tuple-element.27), channel_id=1, source_target_pairs={{0,2},{2,4},{4,6},{6,8},{8,10},{10,12},{12,14},{14,16},{16,18},{18... | collective-permute-start | bytes 99848 | tf_op jit(solution)/shard_map/ppermute | solution.py:24
  12.0 2.5 %copy-start = (f32[2,16,8,128]{3,2,1,0:T(8,128)S(1)}, f32[2,16,8,128]{3,2,1,0:T(8,128)}, u32[]{:S(2)}) copy-start(f32[2,16,8,128]{3,2,1,0:T(8,128)} %param.5) | copy-start | bytes 393220
  12.0 2.5 %copy-start.1 = (f32[2,16,8,128]{3,2,1,0:T(8,128)S(1)}, f32[2,16,8,128]{3,2,1,0:T(8,128)}, u32[]{:S(2)}) copy-start(f32[2,16,8,128]{3,2,1,0:T(8,128)} %param.4) | copy-start | bytes 393220
  12.4 4.1 %collective-permute-start.4 = (f32[65,10,1]{0,2,1:T(1,128)S(1)}, f32[65,10,1]{0,2,1:T(1,128)S(1)}, u32[]{:S(2)}, u32[]{:S(2)}) collective-permute-start(f32[65,10,1]{0,2,1:T(1,128)S(1)} %copy.31), channel_id=1, source_target_pairs={{1,0},{0,1},{3,2},{2,3},{5,4},{4,5},{7,6},{6,7},{9,8},{8,9},{11,10... | collective-permute-start | bytes 7808 | tf_op jit(solution)/shard_map/ppermute | solution.py:26
  12.5 3.7 %collective-permute-start.3 = (f32[65,10,1]{0,2,1:T(1,128)S(1)}, f32[65,10,1]{0,2,1:T(1,128)S(1)}, u32[]{:S(2)}, u32[]{:S(2)}) collective-permute-start(f32[65,10,1]{0,2,1:T(1,128)S(1)} %copy.30), channel_id=1, source_target_pairs={{0,1},{1,0},{2,3},{3,2},{4,5},{5,4},{6,7},{7,6},{8,9},{9,8},{10,11... | collective-permute-start | bytes 7808 | tf_op jit(solution)/shard_map/ppermute | solution.py:24
  17.8 9.8 %collective-permute-start.5 = (f32[1,1,128]{2,1,0:T(1,128)S(1)}, f32[1,1,128]{2,1,0:T(1,128)S(1)}, u32[]{:S(2)}, u32[]{:S(2)}) collective-permute-start(f32[1,1,128]{2,1,0:T(1,128)S(1)} %get-tuple-element.43), channel_id=1, source_target_pairs={{0,2},{2,4},{4,6},{6,8},{8,10},{10,12},{12,14},{14,16},{16,18},{18... | collective-permute-start | bytes 1544 | tf_op jit(solution)/shard_map/ppermute | solution.py:24
  19.9 5.2 %collective-permute-start.6 = (f32[1,128]{1,0:T(1,128)S(1)}, f32[1,128]{1,0:T(1,128)S(1)}, u32[]{:S(2)}, u32[]{:S(2)}) collective-permute-start(f32[1,128]{1,0:T(1,128)S(1)} %get-tuple-element.44), channel_id=1, source_target_pairs={{0,1},{1,0},{2,3},{3,2},{4,5},{5,4},{6,7},{7,6},{8,9},{9,8},{10,11... | collective-permute-start | bytes 1544 | tf_op jit(solution)/shard_map/ppermute | solution.py:13
  21.8 5.7 %collective-permute-start.7 = (f32[1,1,128]{2,1,0:T(1,128)S(1)}, f32[1,1,128]{2,1,0:T(1,128)S(1)}, u32[]{:S(2)}, u32[]{:S(2)}) collective-permute-start(f32[1,1,128]{2,1,0:T(1,128)S(1)} %get-tuple-element.45), channel_id=1, source_target_pairs={{2,0},{4,2},{6,4},{8,6},{10,8},{12,10},{14,12},{16,14},{18,16},{20... | collective-permute-start | bytes 1544 | tf_op jit(solution)/shard_map/ppermute | solution.py:26
  24.3 0.7 copy-start.2
  27.6 3.7 %collective-permute-start.8 = (f32[1,10,1]{2,1,0:T(8,128)S(1)}, f32[1,10,1]{2,1,0:T(8,128)S(1)}, u32[]{:S(2)}, u32[]{:S(2)}) collective-permute-start(f32[1,10,1]{2,1,0:T(8,128)S(1)} %get-tuple-element.33), channel_id=1, source_target_pairs={{0,1},{1,0},{2,3},{3,2},{4,5},{5,4},{6,7},{7,6},{8,9},{9,8},{10,11... | collective-permute-start | bytes 128 | tf_op jit(solution)/shard_map/ppermute | solution.py:24
  28.2 3.7 %collective-permute-start.9 = (f32[1,10,1]{2,1,0:T(8,128)S(1)}, f32[1,10,1]{2,1,0:T(8,128)S(1)}, u32[]{:S(2)}, u32[]{:S(2)}) collective-permute-start(f32[1,10,1]{2,1,0:T(8,128)S(1)} %get-tuple-element.34), channel_id=1, source_target_pairs={{1,0},{0,1},{3,2},{2,3},{5,4},{4,5},{7,6},{6,7},{9,8},{8,9},{11,10... | collective-permute-start | bytes 128 | tf_op jit(solution)/shard_map/ppermute | solution.py:26
  77.6 6.9 %collective-permute-start.11 = (f32[1,128]{1,0:T(1,128)S(1)}, f32[1,128]{1,0:T(1,128)S(1)}, u32[]{:S(2)}, u32[]{:S(2)}) collective-permute-start(f32[1,128]{1,0:T(1,128)S(1)} %get-tuple-element.41), channel_id=1, source_target_pairs={{0,1},{1,0},{2,3},{3,2},{4,5},{5,4},{6,7},{7,6},{8,9},{9,8},{10,11... | collective-permute-start | bytes 1544 | tf_op jit(solution)/shard_map/ppermute | solution.py:13
  80.0 4.7 %collective-permute-start.12 = (f32[1,1,128]{2,1,0:T(1,128)S(1)}, f32[1,1,128]{2,1,0:T(1,128)S(1)}, u32[]{:S(2)}, u32[]{:S(2)}) collective-permute-start(f32[1,1,128]{2,1,0:T(1,128)S(1)} %get-tuple-element.42), channel_id=1, source_target_pairs={{2,0},{4,2},{6,4},{8,6},{10,8},{12,10},{14,12},{16,14},{18,16},{20... | collective-permute-start | bytes 1544 | tf_op jit(solution)/shard_map/ppermute | solution.py:26
  81.5 3.8 %collective-permute-start.10 = (f32[1,1,128]{2,1,0:T(1,128)S(1)}, f32[1,1,128]{2,1,0:T(1,128)S(1)}, u32[]{:S(2)}, u32[]{:S(2)}) collective-permute-start(f32[1,1,128]{2,1,0:T(1,128)S(1)} %get-tuple-element.40), channel_id=1, source_target_pairs={{0,2},{2,4},{4,6},{6,8},{8,10},{10,12},{12,14},{14,16},{16,18},{18... | collective-permute-start | bytes 1544 | tf_op jit(solution)/shard_map/ppermute | solution.py:24
  85.4 3.7 %collective-permute-start.13 = (f32[1,10,1]{2,1,0:T(8,128)S(1)}, f32[1,10,1]{2,1,0:T(8,128)S(1)}, u32[]{:S(2)}, u32[]{:S(2)}) collective-permute-start(f32[1,10,1]{2,1,0:T(8,128)S(1)} %get-tuple-element.31), channel_id=1, source_target_pairs={{0,1},{1,0},{2,3},{3,2},{4,5},{5,4},{6,7},{7,6},{8,9},{9,8},{10,11... | collective-permute-start | bytes 128 | tf_op jit(solution)/shard_map/ppermute | solution.py:24
  85.5 3.7 %collective-permute-start.14 = (f32[1,10,1]{2,1,0:T(8,128)S(1)}, f32[1,10,1]{2,1,0:T(8,128)S(1)}, u32[]{:S(2)}, u32[]{:S(2)}) collective-permute-start(f32[1,10,1]{2,1,0:T(8,128)S(1)} %get-tuple-element.32), channel_id=1, source_target_pairs={{1,0},{0,1},{3,2},{2,3},{5,4},{4,5},{7,6},{6,7},{9,8},{8,9},{11,10... | collective-permute-start | bytes 128 | tf_op jit(solution)/shard_map/ppermute | solution.py:26
  137.4 7.5 %collective-permute-start.16 = (f32[1,128]{1,0:T(1,128)S(1)}, f32[1,128]{1,0:T(1,128)S(1)}, u32[]{:S(2)}, u32[]{:S(2)}) collective-permute-start(f32[1,128]{1,0:T(1,128)S(1)} %get-tuple-element.38), channel_id=1, source_target_pairs={{0,1},{1,0},{2,3},{3,2},{4,5},{5,4},{6,7},{7,6},{8,9},{9,8},{10,11... | collective-permute-start | bytes 1544 | tf_op jit(solution)/shard_map/ppermute | solution.py:13
  139.7 5.3 %collective-permute-start.17 = (f32[1,1,128]{2,1,0:T(1,128)S(1)}, f32[1,1,128]{2,1,0:T(1,128)S(1)}, u32[]{:S(2)}, u32[]{:S(2)}) collective-permute-start(f32[1,1,128]{2,1,0:T(1,128)S(1)} %get-tuple-element.39), channel_id=1, source_target_pairs={{2,0},{4,2},{6,4},{8,6},{10,8},{12,10},{14,12},{16,14},{18,16},{20... | collective-permute-start | bytes 1544 | tf_op jit(solution)/shard_map/ppermute | solution.py:26
  141.9 3.8 %collective-permute-start.15 = (f32[1,1,128]{2,1,0:T(1,128)S(1)}, f32[1,1,128]{2,1,0:T(1,128)S(1)}, u32[]{:S(2)}, u32[]{:S(2)}) collective-permute-start(f32[1,1,128]{2,1,0:T(1,128)S(1)} %get-tuple-element.37), channel_id=1, source_target_pairs={{0,2},{2,4},{4,6},{6,8},{8,10},{10,12},{12,14},{14,16},{16,18},{18... | collective-permute-start | bytes 1544 | tf_op jit(solution)/shard_map/ppermute | solution.py:24
  145.8 3.7 %collective-permute-start.18 = (f32[1,10,1]{2,1,0:T(8,128)S(1)}, f32[1,10,1]{2,1,0:T(8,128)S(1)}, u32[]{:S(2)}, u32[]{:S(2)}) collective-permute-start(f32[1,10,1]{2,1,0:T(8,128)S(1)} %get-tuple-element.29), channel_id=1, source_target_pairs={{0,1},{1,0},{2,3},{3,2},{4,5},{5,4},{6,7},{7,6},{8,9},{9,8},{10,11... | collective-permute-start | bytes 128 | tf_op jit(solution)/shard_map/ppermute | solution.py:24
  145.8 3.8 %collective-permute-start.19 = (f32[1,10,1]{2,1,0:T(8,128)S(1)}, f32[1,10,1]{2,1,0:T(8,128)S(1)}, u32[]{:S(2)}, u32[]{:S(2)}) collective-permute-start(f32[1,10,1]{2,1,0:T(8,128)S(1)} %get-tuple-element.30), channel_id=1, source_target_pairs={{1,0},{0,1},{3,2},{2,3},{5,4},{4,5},{7,6},{6,7},{9,8},{8,9},{11,10... | collective-permute-start | bytes 128 | tf_op jit(solution)/shard_map/ppermute | solution.py:26
where the time goes:
time: 198 us; the launch traced here: 197 us
  blocking collectives  129 us (65%)
  starting transfers between devices  34.1 us (17%)
  between operations  11.1 us (6%)
  waiting for transfers between devices  10.9 us (6%)
  other arithmetic  9.03 us (5%)
  local copies, waits for them, and re-layouts  3.44 us (2%)
    psum x3, blocking collectives, two_sums(): lax.psum((jnp.sum(residual * residual), jnp.sum(residual * applied)), ('b...  129 us
    ppermute x8, starting transfers between devices, padded_2(): lax.ppermute(tail, axis, [(i, (i + 1) % count) for i in range(ends)])  13.9 us
    ppermute x8, starting transfers between devices, padded_2(): lax.ppermute(head, axis, [((i + 1) % count, i) for i in range(ends)])  10.7 us
    ppermute x4, starting transfers between devices, swapped(): lax.ppermute(value, axis, [(i, i ^ 1 << stride) for i in range(lax.axis_s...  9.6 us
    ppermute x8, waiting for transfers between devices, padded_2(): lax.ppermute(tail, axis, [(i, (i + 1) % count) for i in range(ends)])  7.85 us
  transfers between devices with their start and end apart: 20, of which 10 were waited for; matrix products, arithmetic and copies ran while one was open for 2% of the time, Pallas kernels for 0%

commit v1 on v0

--- a/solution.py
+++ b/solution.py
@@ -112,7 +112,9 @@
 
 
 def two_sums(residual, applied):
-    return lax.psum((jnp.sum(residual * residual), jnp.sum(residual * applied)), ("blk", "grp"))
+    return lax.psum(
+        lax.psum((jnp.sum(residual * residual), jnp.sum(residual * applied)), "grp"), "blk"
+    )
 
 
 def shards(tracers, velocity, depth_levels, vdiff):

time: 198 us -> 178 us (0.90)
  blocking collectives: 129 us -> 109 us
    psum x3 -> x6, blocking collectives: 129 us -> 109 us  [the longest x3 92.6 us: two_sums(): lax.psum(lax.psum((jnp.sum(residual * residual), jnp.sum(residual * appli...]
where the time goes in v1:
time: 178 us; the launch traced here: 177 us
  blocking collectives  109 us (61%)
  starting transfers between devices  32.6 us (18%)
  waiting for transfers between devices  11.7 us (7%)
  between operations  10.9 us (6%)
  other arithmetic  9.1 us (5%)
  local copies, waits for them, and re-layouts  3.44 us (2%)
    psum x3, blocking collectives, two_sums(): lax.psum(lax.psum((jnp.sum(residual * residual), jnp.sum(residual * appli...  92.6 us
    psum x3, blocking collectives, two_sums(): lax.psum((jnp.sum(residual * residual), jnp.sum(residual * applied)), 'grp')  16.7 us
    ppermute x8, starting transfers between devices, padded_2(): lax.ppermute(tail, axis, [(i, (i + 1) % count) for i in range(ends)])  14.9 us
    ppermute x8, starting transfers between devices, padded_2(): lax.ppermute(head, axis, [((i + 1) % count, i) for i in range(ends)])  9.69 us
    ppermute x4, starting transfers between devices, swapped(): lax.ppermute(value, axis, [(i, i ^ 1 << stride) for i in range(lax.axis_s...  8.06 us
    ppermute x8, waiting for transfers between devices, padded_2(): lax.ppermute(tail, axis, [(i, (i + 1) % count) for i in range(ends)])  7.93 us
    ppermute x8, waiting for transfers between devices, padded_2(): lax.ppermute(head, axis, [((i + 1) % count, i) for i in range(ends)])  3.79 us
  transfers between devices with their start and end apart: 20, of which 10 were waited for; matrix products, arithmetic and copies ran while one was open for 2% of the time, Pallas kernels for 0%

profile of v1, /device:TPU:0, one launch (start us, length us, event | category | flops | bytes accessed | tf_op | source)
XLA Modules:
  0.0 177.0 jit_solution(1138090509801742430)
XLA Ops:
  0.6 0.7 convert_bitcast_fusion
  1.3 1.1 pad_maximum_fusion.20
  2.5 3.0 %collective-permute-start.1 = (f32[65,128]{1,0:T(8,128)S(1)}, f32[65,128]{1,0:T(8,128)S(1)}, u32[]{:S(2)}, u32[]{:S(2)}) collective-permute-start(f32[65,128]{1,0:T(8,128)S(1)} %bitcast.70), channel_id=1, source_target_pairs={{0,1},{1,0},{2,3},{3,2},{4,5},{5,4},{6,7},{7,6},{8,9},{9,8},{10,11... | collective-permute-start | bytes 99848 | tf_op jit(solution)/shard_map/ppermute | solution.py:13
  5.5 1.3 collective-permute-start.2
  6.8 3.0 %collective-permute-start = (f32[65,1,128]{2,1,0:T(1,128)S(1)}, f32[65,1,128]{2,1,0:T(1,128)S(1)}, u32[]{:S(2)}, u32[]{:S(2)}) collective-permute-start(f32[65,1,128]{2,1,0:T(1,128)S(1)} %get-tuple-element.33), channel_id=1, source_target_pairs={{0,2},{2,4},{4,6},{6,8},{8,10},{10,12},{12,14},{14,16},{16,18},{18... | collective-permute-start | bytes 99848 | tf_op jit(solution)/shard_map/ppermute | solution.py:24
  9.9 0.7 fusion.14
  10.7 1.1 pad_maximum_fusion.1
  11.8 0.2 fusion.58
  12.0 0.2 copy.30
  12.2 0.2 copy.31
  12.5 2.0 %collective-permute-start.3 = (f32[65,10,1]{0,2,1:T(1,128)S(1)}, f32[65,10,1]{0,2,1:T(1,128)S(1)}, u32[]{:S(2)}, u32[]{:S(2)}) collective-permute-start(f32[65,10,1]{0,2,1:T(1,128)S(1)} %copy.30), channel_id=1, source_target_pairs={{0,1},{1,0},{2,3},{3,2},{4,5},{5,4},{6,7},{7,6},{8,9},{9,8},{10,11... | collective-permute-start | bytes 7808 | tf_op jit(solution)/shard_map/ppermute | solution.py:24
  14.6 1.6 collective-permute-done.3
  16.2 0.3 copy.32
  16.5 0.3 copy.33
  17.0 0.1 slice_multiply_fusion
  17.1 0.1 slice_multiply_fusion.1
  17.2 0.4 fusion.1
  17.8 2.2 %collective-permute-start.5 = (f32[1,1,128]{2,1,0:T(1,128)S(1)}, f32[1,1,128]{2,1,0:T(1,128)S(1)}, u32[]{:S(2)}, u32[]{:S(2)}) collective-permute-start(f32[1,1,128]{2,1,0:T(1,128)S(1)} %get-tuple-element.49), channel_id=1, source_target_pairs={{0,2},{2,4},{4,6},{6,8},{8,10},{10,12},{12,14},{14,16},{16,18},{18... | collective-permute-start | bytes 1544 | tf_op jit(solution)/shard_map/ppermute | solution.py:24
  19.9 1.9 %collective-permute-start.6 = (f32[1,128]{1,0:T(1,128)S(1)}, f32[1,128]{1,0:T(1,128)S(1)}, u32[]{:S(2)}, u32[]{:S(2)}) collective-permute-start(f32[1,128]{1,0:T(1,128)S(1)} %get-tuple-element.50), channel_id=1, source_target_pairs={{0,1},{1,0},{2,3},{3,2},{4,5},{5,4},{6,7},{7,6},{8,9},{9,8},{10,11... | collective-permute-start | bytes 1544 | tf_op jit(solution)/shard_map/ppermute | solution.py:13
  21.8 1.3 collective-permute-start.7
  23.1 0.8 pad_maximum_fusion
  23.9 0.2 copy.35
  24.1 0.1 fusion.11
  24.4 0.1 subtract_multiply_fusion.1
  24.6 0.1 subtract_multiply_fusion
  24.7 0.3 copy-done.2
  25.0 0.1 fusion.13
  25.1 0.1 rev.13
  25.2 2.3 %collective-permute-done.7 = f32[1,1,128]{2,1,0:T(1,128)S(1)} collective-permute-done((f32[1,1,128]{2,1,0:T(1,128)S(1)}, f32[1,1,128]{2,1,0:T(1,128)S(1)}, u32[]{:S(2)}, u32[]{:S(2)}) %collective-permute-start.7) | collective-permute-done | bytes 544 | tf_op jit(solution)/shard_map/ppermute | solution.py:26
  27.6 0.5 collective-permute-start.8
  28.2 1.5 collective-permute-start.9
  29.6 1.6 collective-permute-done.8
  31.3 0.5 collective-permute-done.9
  31.9 0.7 multiply_reduce_fusion.4
  32.6 5.5 %all-reduce.7 = (f32[]{:T(128)}, f32[]{:T(128)}) all-reduce(f32[]{:T(128)} %get-tuple-element.13, f32[]{:T(128)} %get-tuple-element.12), channel_id=1, replica_groups=mesh['blk'=16,'grp'=2] {'grp'}, use_global_device_ids=true, to_apply=%region_3.4 | all-reduce | flops 2 | bytes 16 | tf_op jit(solution)/shard_map/psum | solution.py:116
  38.1 32.3 %all-reduce.4 = (f32[]{:T(128)}, f32[]{:T(128)}) all-reduce(f32[]{:T(128)} %get-tuple-element.24, f32[]{:T(128)} %get-tuple-element.25), channel_id=1, replica_groups=mesh['blk'=16,'grp'=2] {'blk'}, use_global_device_ids=true, to_apply=%region_4.5 | all-reduce | flops 2 | bytes 16 | tf_op jit(solution)/shard_map/psum | solution.py:115
  71.8 1.6 collective-permute-start.11
  73.4 1.3 collective-permute-start.12
  74.7 0.1 fusion.12
  74.9 3.0 %collective-permute-start.10 = (f32[1,1,128]{2,1,0:T(1,128)S(1)}, f32[1,1,128]{2,1,0:T(1,128)S(1)}, u32[]{:S(2)}, u32[]{:S(2)}) collective-permute-start(f32[1,1,128]{2,1,0:T(1,128)S(1)} %get-tuple-element.46), channel_id=1, source_target_pairs={{0,2},{2,4},{4,6},{6,8},{8,10},{10,12},{12,14},{14,16},{16,18},{18... | collective-permute-start | bytes 1544 | tf_op jit(solution)/shard_map/ppermute | solution.py:24
  78.0 0.1 rev.14
  78.1 0.7 collective-permute-done.10
  78.8 0.5 collective-permute-start.13
  79.4 1.5 collective-permute-start.14
  80.9 1.6 collective-permute-done.13
  82.5 0.5 collective-permute-done.14
  83.1 0.8 multiply_reduce_fusion.2
  83.8 5.6 %all-reduce.6 = (f32[]{:T(128)}, f32[]{:T(128)}) all-reduce(f32[]{:T(128)} %get-tuple-element.11, f32[]{:T(128)} %get-tuple-element.10), channel_id=1, replica_groups=mesh['blk'=16,'grp'=2] {'grp'}, use_global_device_ids=true, to_apply=%region_9.10 | all-reduce | flops 2 | bytes 16 | tf_op jit(solution)/shard_map/psum | solution.py:116
  89.4 30.2 %all-reduce.3 = (f32[]{:T(128)}, f32[]{:T(128)}) all-reduce(f32[]{:T(128)} %get-tuple-element.22, f32[]{:T(128)} %get-tuple-element.23), channel_id=1, replica_groups=mesh['blk'=16,'grp'=2] {'blk'}, use_global_device_ids=true, to_apply=%region_10.11 | all-reduce | flops 2 | bytes 16 | tf_op jit(solution)/shard_map/psum | solution.py:115
  124.2 1.6 collective-permute-start.16
  125.8 1.3 collective-permute-start.17
  127.0 0.1 fusion.6
  127.2 0.7 copy.44
  127.9 3.0 %collective-permute-start.15 = (f32[1,1,128]{2,1,0:T(1,128)S(1)}, f32[1,1,128]{2,1,0:T(1,128)S(1)}, u32[]{:S(2)}, u32[]{:S(2)}) collective-permute-start(f32[1,1,128]{2,1,0:T(1,128)S(1)} %get-tuple-element.43), channel_id=1, source_target_pairs={{0,2},{2,4},{4,6},{6,8},{8,10},{10,12},{12,14},{14,16},{16,18},{18... | collective-permute-start | bytes 1544 | tf_op jit(solution)/shard_map/ppermute | solution.py:24
  131.0 0.1 rev.15
  131.1 0.7 collective-permute-done.15
  131.8 0.5 collective-permute-start.18
  132.4 1.5 collective-permute-start.19
  133.9 1.7 collective-permute-done.18
  135.6 0.4 collective-permute-done.19
  136.1 0.7 multiply_reduce_fusion
  136.8 5.5 %all-reduce.5 = (f32[]{:T(128)}, f32[]{:T(128)}) all-reduce(f32[]{:T(128)} %get-tuple-element.9, f32[]{:T(128)} %get-tuple-element.8), channel_id=1, replica_groups=mesh['blk'=16,'grp'=2] {'grp'}, use_global_device_ids=true, to_apply=%region_15.16 | all-reduce | flops 2 | bytes 16 | tf_op jit(solution)/shard_map/psum | solution.py:116
  142.3 30.1 %all-reduce.2 = (f32[]{:T(128)}, f32[]{:T(128)}) all-reduce(f32[]{:T(128)} %get-tuple-element.20, f32[]{:T(128)} %get-tuple-element.21), channel_id=1, replica_groups=mesh['blk'=16,'grp'=2] {'blk'}, use_global_device_ids=true, to_apply=%region_16.17 | all-reduce | flops 2 | bytes 16 | tf_op jit(solution)/shard_map/psum | solution.py:115
  176.4 0.6 multiply_subtract_fusion
  (49 shorter events, 1.3 us)
Async XLA Ops:
  2.5 7.4 %collective-permute-start.1 = (f32[65,128]{1,0:T(8,128)S(1)}, f32[65,128]{1,0:T(8,128)S(1)}, u32[]{:S(2)}, u32[]{:S(2)}) collective-permute-start(f32[65,128]{1,0:T(8,128)S(1)} %bitcast.70), channel_id=1, source_target_pairs={{0,1},{1,0},{2,3},{3,2},{4,5},{5,4},{6,7},{7,6},{8,9},{9,8},{10,11... | collective-permute-start | bytes 99848 | tf_op jit(solution)/shard_map/ppermute | solution.py:13
  5.5 4.4 %collective-permute-start.2 = (f32[65,1,128]{2,0,1:T(8,128)S(1)}, f32[65,1,128]{2,0,1:T(8,128)S(1)}, u32[]{:S(2)}, u32[]{:S(2)}) collective-permute-start(f32[65,1,128]{2,0,1:T(8,128)S(1)} %copy.46), channel_id=1, source_target_pairs={{2,0},{4,2},{6,4},{8,6},{10,8},{12,10},{14,12},{16,14},{18,16},{20... | collective-permute-start | bytes 99848 | tf_op jit(solution)/shard_map/ppermute | solution.py:26
  6.8 3.9 %collective-permute-start = (f32[65,1,128]{2,1,0:T(1,128)S(1)}, f32[65,1,128]{2,1,0:T(1,128)S(1)}, u32[]{:S(2)}, u32[]{:S(2)}) collective-permute-start(f32[65,1,128]{2,1,0:T(1,128)S(1)} %get-tuple-element.33), channel_id=1, source_target_pairs={{0,2},{2,4},{4,6},{6,8},{8,10},{10,12},{12,14},{14,16},{16,18},{18... | collective-permute-start | bytes 99848 | tf_op jit(solution)/shard_map/ppermute | solution.py:24
  12.0 2.5 %copy-start = (f32[2,16,8,128]{3,2,1,0:T(8,128)S(1)}, f32[2,16,8,128]{3,2,1,0:T(8,128)}, u32[]{:S(2)}) copy-start(f32[2,16,8,128]{3,2,1,0:T(8,128)} %param.5) | copy-start | bytes 393220
  12.0 2.5 %copy-start.1 = (f32[2,16,8,128]{3,2,1,0:T(8,128)S(1)}, f32[2,16,8,128]{3,2,1,0:T(8,128)}, u32[]{:S(2)}) copy-start(f32[2,16,8,128]{3,2,1,0:T(8,128)} %param.4) | copy-start | bytes 393220
  12.4 4.1 %collective-permute-start.4 = (f32[65,10,1]{0,2,1:T(1,128)S(1)}, f32[65,10,1]{0,2,1:T(1,128)S(1)}, u32[]{:S(2)}, u32[]{:S(2)}) collective-permute-start(f32[65,10,1]{0,2,1:T(1,128)S(1)} %copy.31), channel_id=1, source_target_pairs={{1,0},{0,1},{3,2},{2,3},{5,4},{4,5},{7,6},{6,7},{9,8},{8,9},{11,10... | collective-permute-start | bytes 7808 | tf_op jit(solution)/shard_map/ppermute | solution.py:26
  12.5 3.7 %collective-permute-start.3 = (f32[65,10,1]{0,2,1:T(1,128)S(1)}, f32[65,10,1]{0,2,1:T(1,128)S(1)}, u32[]{:S(2)}, u32[]{:S(2)}) collective-permute-start(f32[65,10,1]{0,2,1:T(1,128)S(1)} %copy.30), channel_id=1, source_target_pairs={{0,1},{1,0},{2,3},{3,2},{4,5},{5,4},{6,7},{7,6},{8,9},{9,8},{10,11... | collective-permute-start | bytes 7808 | tf_op jit(solution)/shard_map/ppermute | solution.py:24
  17.8 9.8 %collective-permute-start.5 = (f32[1,1,128]{2,1,0:T(1,128)S(1)}, f32[1,1,128]{2,1,0:T(1,128)S(1)}, u32[]{:S(2)}, u32[]{:S(2)}) collective-permute-start(f32[1,1,128]{2,1,0:T(1,128)S(1)} %get-tuple-element.49), channel_id=1, source_target_pairs={{0,2},{2,4},{4,6},{6,8},{8,10},{10,12},{12,14},{14,16},{16,18},{18... | collective-permute-start | bytes 1544 | tf_op jit(solution)/shard_map/ppermute | solution.py:24
  19.9 5.2 %collective-permute-start.6 = (f32[1,128]{1,0:T(1,128)S(1)}, f32[1,128]{1,0:T(1,128)S(1)}, u32[]{:S(2)}, u32[]{:S(2)}) collective-permute-start(f32[1,128]{1,0:T(1,128)S(1)} %get-tuple-element.50), channel_id=1, source_target_pairs={{0,1},{1,0},{2,3},{3,2},{4,5},{5,4},{6,7},{7,6},{8,9},{9,8},{10,11... | collective-permute-start | bytes 1544 | tf_op jit(solution)/shard_map/ppermute | solution.py:13
  21.8 5.7 %collective-permute-start.7 = (f32[1,1,128]{2,1,0:T(1,128)S(1)}, f32[1,1,128]{2,1,0:T(1,128)S(1)}, u32[]{:S(2)}, u32[]{:S(2)}) collective-permute-start(f32[1,1,128]{2,1,0:T(1,128)S(1)} %get-tuple-element.51), channel_id=1, source_target_pairs={{2,0},{4,2},{6,4},{8,6},{10,8},{12,10},{14,12},{16,14},{18,16},{20... | collective-permute-start | bytes 1544 | tf_op jit(solution)/shard_map/ppermute | solution.py:26
  24.3 0.7 copy-start.2
  27.6 3.7 %collective-permute-start.8 = (f32[1,10,1]{2,1,0:T(8,128)S(1)}, f32[1,10,1]{2,1,0:T(8,128)S(1)}, u32[]{:S(2)}, u32[]{:S(2)}) collective-permute-start(f32[1,10,1]{2,1,0:T(8,128)S(1)} %get-tuple-element.39), channel_id=1, source_target_pairs={{0,1},{1,0},{2,3},{3,2},{4,5},{5,4},{6,7},{7,6},{8,9},{9,8},{10,11... | collective-permute-start | bytes 128 | tf_op jit(solution)/shard_map/ppermute | solution.py:24
  28.2 3.7 %collective-permute-start.9 = (f32[1,10,1]{2,1,0:T(8,128)S(1)}, f32[1,10,1]{2,1,0:T(8,128)S(1)}, u32[]{:S(2)}, u32[]{:S(2)}) collective-permute-start(f32[1,10,1]{2,1,0:T(8,128)S(1)} %get-tuple-element.40), channel_id=1, source_target_pairs={{1,0},{0,1},{3,2},{2,3},{5,4},{4,5},{7,6},{6,7},{9,8},{8,9},{11,10... | collective-permute-start | bytes 128 | tf_op jit(solution)/shard_map/ppermute | solution.py:26
  71.8 6.1 %collective-permute-start.11 = (f32[1,128]{1,0:T(1,128)S(1)}, f32[1,128]{1,0:T(1,128)S(1)}, u32[]{:S(2)}, u32[]{:S(2)}) collective-permute-start(f32[1,128]{1,0:T(1,128)S(1)} %get-tuple-element.47), channel_id=1, source_target_pairs={{0,1},{1,0},{2,3},{3,2},{4,5},{5,4},{6,7},{7,6},{8,9},{9,8},{10,11... | collective-permute-start | bytes 1544 | tf_op jit(solution)/shard_map/ppermute | solution.py:13
  73.4 4.7 %collective-permute-start.12 = (f32[1,1,128]{2,1,0:T(1,128)S(1)}, f32[1,1,128]{2,1,0:T(1,128)S(1)}, u32[]{:S(2)}, u32[]{:S(2)}) collective-permute-start(f32[1,1,128]{2,1,0:T(1,128)S(1)} %get-tuple-element.48), channel_id=1, source_target_pairs={{2,0},{4,2},{6,4},{8,6},{10,8},{12,10},{14,12},{16,14},{18,16},{20... | collective-permute-start | bytes 1544 | tf_op jit(solution)/shard_map/ppermute | solution.py:26
  74.9 3.8 %collective-permute-start.10 = (f32[1,1,128]{2,1,0:T(1,128)S(1)}, f32[1,1,128]{2,1,0:T(1,128)S(1)}, u32[]{:S(2)}, u32[]{:S(2)}) collective-permute-start(f32[1,1,128]{2,1,0:T(1,128)S(1)} %get-tuple-element.46), channel_id=1, source_target_pairs={{0,2},{2,4},{4,6},{6,8},{8,10},{10,12},{12,14},{14,16},{16,18},{18... | collective-permute-start | bytes 1544 | tf_op jit(solution)/shard_map/ppermute | solution.py:24
  78.8 3.7 %collective-permute-start.13 = (f32[1,10,1]{2,1,0:T(8,128)S(1)}, f32[1,10,1]{2,1,0:T(8,128)S(1)}, u32[]{:S(2)}, u32[]{:S(2)}) collective-permute-start(f32[1,10,1]{2,1,0:T(8,128)S(1)} %get-tuple-element.37), channel_id=1, source_target_pairs={{0,1},{1,0},{2,3},{3,2},{4,5},{5,4},{6,7},{7,6},{8,9},{9,8},{10,11... | collective-permute-start | bytes 128 | tf_op jit(solution)/shard_map/ppermute | solution.py:24
  79.4 3.7 %collective-permute-start.14 = (f32[1,10,1]{2,1,0:T(8,128)S(1)}, f32[1,10,1]{2,1,0:T(8,128)S(1)}, u32[]{:S(2)}, u32[]{:S(2)}) collective-permute-start(f32[1,10,1]{2,1,0:T(8,128)S(1)} %get-tuple-element.38), channel_id=1, source_target_pairs={{1,0},{0,1},{3,2},{2,3},{5,4},{4,5},{7,6},{6,7},{9,8},{8,9},{11,10... | collective-permute-start | bytes 128 | tf_op jit(solution)/shard_map/ppermute | solution.py:26
  124.2 6.8 %collective-permute-start.16 = (f32[1,128]{1,0:T(1,128)S(1)}, f32[1,128]{1,0:T(1,128)S(1)}, u32[]{:S(2)}, u32[]{:S(2)}) collective-permute-start(f32[1,128]{1,0:T(1,128)S(1)} %get-tuple-element.44), channel_id=1, source_target_pairs={{0,1},{1,0},{2,3},{3,2},{4,5},{5,4},{6,7},{7,6},{8,9},{9,8},{10,11... | collective-permute-start | bytes 1544 | tf_op jit(solution)/shard_map/ppermute | solution.py:13
  125.8 5.3 %collective-permute-start.17 = (f32[1,1,128]{2,1,0:T(1,128)S(1)}, f32[1,1,128]{2,1,0:T(1,128)S(1)}, u32[]{:S(2)}, u32[]{:S(2)}) collective-permute-start(f32[1,1,128]{2,1,0:T(1,128)S(1)} %get-tuple-element.45), channel_id=1, source_target_pairs={{2,0},{4,2},{6,4},{8,6},{10,8},{12,10},{14,12},{16,14},{18,16},{20... | collective-permute-start | bytes 1544 | tf_op jit(solution)/shard_map/ppermute | solution.py:26
  127.9 3.8 %collective-permute-start.15 = (f32[1,1,128]{2,1,0:T(1,128)S(1)}, f32[1,1,128]{2,1,0:T(1,128)S(1)}, u32[]{:S(2)}, u32[]{:S(2)}) collective-permute-start(f32[1,1,128]{2,1,0:T(1,128)S(1)} %get-tuple-element.43), channel_id=1, source_target_pairs={{0,2},{2,4},{4,6},{6,8},{8,10},{10,12},{12,14},{14,16},{16,18},{18... | collective-permute-start | bytes 1544 | tf_op jit(solution)/shard_map/ppermute | solution.py:24
  131.8 3.7 %collective-permute-start.18 = (f32[1,10,1]{2,1,0:T(8,128)S(1)}, f32[1,10,1]{2,1,0:T(8,128)S(1)}, u32[]{:S(2)}, u32[]{:S(2)}) collective-permute-start(f32[1,10,1]{2,1,0:T(8,128)S(1)} %get-tuple-element.35), channel_id=1, source_target_pairs={{0,1},{1,0},{2,3},{3,2},{4,5},{5,4},{6,7},{7,6},{8,9},{9,8},{10,11... | collective-permute-start | bytes 128 | tf_op jit(solution)/shard_map/ppermute | solution.py:24
  132.4 3.7 %collective-permute-start.19 = (f32[1,10,1]{2,1,0:T(8,128)S(1)}, f32[1,10,1]{2,1,0:T(8,128)S(1)}, u32[]{:S(2)}, u32[]{:S(2)}) collective-permute-start(f32[1,10,1]{2,1,0:T(8,128)S(1)} %get-tuple-element.36), channel_id=1, source_target_pairs={{1,0},{0,1},{3,2},{2,3},{5,4},{4,5},{7,6},{6,7},{9,8},{8,9},{11,10... | collective-permute-start | bytes 128 | tf_op jit(solution)/shard_map/ppermute | solution.py:26
